TPU v7x, 32 devices: a whole 2x2x4 slice. The times are simulated.
32 devices in a mesh: grid: 32 (over z, y, x, core), freq: 1.
Axes of the slice: x: 2, y: 2, z: 4, core: 2. Of those that a mesh axis runs over, the one named last changes fastest.
Arguments:
- replicas: bfloat16 [2, 16384, 2, 512], P('freq', 'grid'), may hold values from -6 to 6
- csm: bfloat16 [2, 2, 512, 512], P('freq', None, 'grid'), as said below
- inverse: bfloat16 [2, 2, 512, 512], P('freq', None, 'grid'), as said below
Outputs:
- bartlett: float32 [16384], P(('grid', 'freq'))
- mvdr: float32 [16384], P(('grid', 'freq'))
Inputs may be any that keep to these rules, and one draw needn't show every extreme that they name: csm[f, 0] + i csm[f, 1] is Hermitian positive definite for every bin. inverse[f, 0] + i inverse[f, 1] is Hermitian positive definite for every bin.
All inputs are finite; a program needn't handle non-finite values.
Results may differ from a plain program's by a relative error of at most 0.0003.
Values may be sent and summed in bfloat16 or wider, within the bound.
A program may use at most 64 MiB of HBM per device.

v0:
```python
import jax
import jax.numpy as jnp
from jax import lax
from jax.sharding import PartitionSpec as P


def body(replicas, csm, inverse):
    bins, points, _, width = replicas.shape
    real_vec = replicas[:, :, 0, :]
    imag_vec = replicas[:, :, 1, :]
    wide_bf = replicas.reshape(bins, points, 2 * width)

    def add_form(piece):
        real_rows = piece[:, 0]
        imag_rows = piece[:, 1]
        block = jnp.concatenate(
            [
                jnp.concatenate([real_rows, -imag_rows], axis=2),
                jnp.concatenate([imag_rows, real_rows], axis=2),
            ],
            axis=1,
        )
        images = jnp.einsum("fgn,fkn->fgk", wide_bf, block, preferred_element_type=jnp.float32)
        picked = jnp.concatenate([real_vec, imag_vec], axis=2).astype(jnp.float32)
        return jnp.sum(images * picked, axis=2)

    power = add_form(lax.all_gather(csm, "grid", axis=2, tiled=True))
    quad = add_form(lax.all_gather(inverse, "grid", axis=2, tiled=True))
    wide = wide_bf.astype(jnp.float32)
    energy = jnp.sum(wide * wide, axis=2) + 1e-06
    single_b = power / energy
    single_m = energy / quad
    peak_b, peak_m = lax.pmax((jnp.max(single_b, axis=1), jnp.max(single_m, axis=1)), "grid")
    local = jnp.stack(
        [jnp.sum(single_b / peak_b[:, None], axis=0), jnp.sum(single_m / peak_m[:, None], axis=0)]
    )
    total_bins = bins * lax.axis_size("freq")
    whole = lax.psum(local, "freq")
    share = points // lax.axis_size("freq")
    summed = lax.dynamic_slice_in_dim(whole, lax.axis_index("freq") * share, share, 1)
    summed = summed / total_bins
    return (summed[0], summed[1])


def solution(mesh):
    in_specs = (
        P("freq", "grid", None, None),
        P("freq", None, "grid", None),
        P("freq", None, "grid", None),
    )
    out_specs = (P(("grid", "freq")), P(("grid", "freq")))
    return jax.shard_map(body, mesh=mesh, in_specs=in_specs, out_specs=out_specs, check_vma=False)
```

profile of v0, /device:TPU:0, one launch (start us, length us, event | category | flops | bytes accessed | tf_op | source)
XLA Modules:
  0.0 180.4 jit_solution(9429921653503206933)
XLA Ops:
  7.2 0.0 all-gather.3.cloned.1.call-start
  7.2 1.5 copy.9
  8.7 0.0 all-gather.3.cloned.1.call-update
  8.7 0.0 all-gather.5.cloned.1.call-start
  8.7 1.5 copy.12
  10.2 0.0 all-gather.5.cloned.1.call-update
  10.2 0.0 copy-start
  10.2 4.6 %reshape.9 = bf16[2,512,1024]{2,1,0:T(8,128)(2,1)} reshape(bf16[2,512,2,512]{3,2,1,0:T(2,128)(2,1)} %param.3) | data formatting | bytes 4194304 | tf_op jit(solution)/shard_map/reshape | solution.py:11
  14.8 0.0 copy-done
  14.8 4.2 %fusion.28 = (bf16[2,512,1,512]{3,2,1,0:T(2,128)(2,1)}, bf16[2,512,1,512]{3,2,1,0:T(2,128)(2,1)}) fusion(bf16[2,512,2,512]{3,2,1,0:T(2,128)(2,1)S(1)} %copy-done), kind=kLoop, calls=%fused_computation.38 | loop fusion | bytes 4194304 | tf_op jit(solution)/shard_map/slice | solution.py:9
  19.1 4.6 %copy.13 = bf16[2,512,1,512]{1,3,0,2:T(8,128)(2,1)S(1)} copy(bf16[2,512,1,512]{3,2,1,0:T(2,128)(2,1)} %get-tuple-element.6) | data formatting | bytes 2097152
  23.7 5.8 %copy.14 = bf16[2,512,1,512]{1,3,0,2:T(8,128)(2,1)} copy(bf16[2,512,1,512]{3,2,1,0:T(2,128)(2,1)} %get-tuple-element.7) | data formatting | bytes 2097152
  29.5 3.6 %multiply_reduce_fusion = f32[2,512]{1,0:T(2,128)S(1)} fusion(bf16[2,512,2,512]{3,2,1,0:T(2,128)(2,1)S(1)} %copy-done), kind=kLoop, calls=%fused_computation.20 | loop fusion | flops 3144704 | bytes 2101248 | tf_op jit(solution)/shard_map/reduce_sum | solution.py:30
  33.1 36.6 %all-gather.3.cloned.1.call-done = bf16[2,2,512,512]{3,2,0,1:T(8,128)(2,1)} async-done(((bf16[2,2,16,512]{3,2,0,1:T(8,128)(2,1)}), bf16[2,2,512,512]{3,2,0,1:T(8,128)(2,1)}) %all-gather.3.cloned.1.call-update) | async-done | bytes 2097168 | tf_op jit(solution)/shard_map/all_gather | solution.py:27
  69.7 0.0 copy-start.2
  69.7 1.4 fusion.26
  71.2 0.5 copy-done.2
  71.6 0.0 copy-start.3
  71.6 0.0 copy-start.4
  71.6 0.1 slice_bitcast_fusion.2
  71.8 1.4 copy-done.3
  73.2 0.3 copy-done.4
  73.5 2.6 %fusion = f32[2,512]{1,0:T(2,128)S(1)} fusion(bf16[2,512,1024]{2,1,0:T(8,128)(2,1)S(1)} %copy-done.3, bf16[2,512,512]{2,1,0:T(8,128)(2,1)S(1)} %get-tuple-element.5, bf16[2,512,512]{2,1,0:T(8,128)(2,1)S(1)} %get-tuple-element.4, bf16[2,512,512]{2,1,0:T(8,128)(2,1)S(1)} %fusion.26, bf16[2,512,512]{1,2,0:T(8,128)(2,1)S(1)} %bitcast.26, ...), kind=kOutput, calls=%fused_computation.2 | convolution fusion | flops 2170551296 | bytes 7344128 | tf_op jit(solution)/shard_map/fgn,fkn->fgk/dot_general | solution.py:23
  76.1 0.1 divide_reduce_fusion.1
  76.2 39.1 %pmax.14 = f32[2]{0:T(128)S(1)} all-reduce(f32[2]{0:T(128)S(1)} %divide_reduce_fusion.1), channel_id=1, replica_groups=mesh['grid'=32,'freq'=1] {'grid'}, use_global_device_ids=true, to_apply=%region_3.0 | all-reduce | flops 2 | bytes 16 | tf_op jit(solution)/shard_map/pmax | solution.py:33
  115.3 12.4 %all-gather.5.cloned.1.call-done = bf16[2,2,512,512]{3,2,0,1:T(8,128)(2,1)} async-done(((bf16[2,2,16,512]{3,2,0,1:T(8,128)(2,1)}), bf16[2,2,512,512]{3,2,0,1:T(8,128)(2,1)}) %all-gather.5.cloned.1.call-update) | async-done | bytes 2097168 | tf_op jit(solution)/shard_map/all_gather | solution.py:28
  127.7 0.0 copy-start.1
  127.7 1.8 %slice_bitcast_fusion = (bf16[2,512,512]{2,1,0:T(8,128)(2,1)S(1)}, bf16[2,512,512]{2,1,0:T(8,128)(2,1)S(1)}) fusion(bf16[2,2,512,512]{3,2,0,1:T(8,128)(2,1)} %all-gather.5.cloned.1.call-done), kind=kLoop, calls=%fused_computation.22 | loop fusion | bytes 4194304 | tf_op jit(solution)/shard_map/squeeze | solution.py:15
  129.5 0.4 copy-done.1
  129.9 0.0 copy-start.5
  129.9 0.1 fusion.27
  130.0 1.1 copy-done.5
  131.1 2.6 %fusion.1 = f32[2,512]{1,0:T(2,128)S(1)} fusion(bf16[2,512,1024]{2,1,0:T(8,128)(2,1)S(1)} %copy-done.3, bf16[2,512,512]{2,1,0:T(8,128)(2,1)S(1)} %get-tuple-element.9, bf16[2,512,512]{2,1,0:T(8,128)(2,1)S(1)} %get-tuple-element.8, bf16[2,512,512]{2,1,0:T(8,128)(2,1)S(1)} %fusion.27, bf16[2,512,512]{1,2,0:T(8,128)(2,1)S(1)} %bitcast.27, ...), kind=kOutput, calls=%fused_computation.3 | convolution fusion | flops 2170551296 | bytes 7344128 | tf_op jit(solution)/shard_map/fgn,fkn->fgk/dot_general | solution.py:23
  133.7 0.2 fusion.22
  133.9 38.9 %pmax.15 = f32[2]{0:T(128)S(1)} all-reduce(f32[2]{0:T(128)S(1)} %get-tuple-element.3), channel_id=1, replica_groups=mesh['grid'=32,'freq'=1] {'grid'}, use_global_device_ids=true, to_apply=%region_7.0 | all-reduce | flops 2 | bytes 16 | tf_op jit(solution)/shard_map/pmax | solution.py:33
  172.8 0.1 fusion.23
  172.9 0.6 fusion.29
  (1 shorter events, 0.0 us)
Async XLA Ops:
  7.2 62.6 %all-gather.3.cloned.1.call-start = ((), (), s32[]{:S(2)}) async-start(), calls=%async_computation | async-start | bytes 2162688 | tf_op jit(solution)/shard_map/all_gather | solution.py:27
  8.7 119.0 %all-gather.5.cloned.1.call-start = ((), (), s32[]{:S(2)}) async-start(), calls=%async_computation.1 | async-start | bytes 2162688 | tf_op jit(solution)/shard_map/all_gather | solution.py:28
  10.2 4.6 %copy-start = (bf16[2,512,2,512]{3,2,1,0:T(2,128)(2,1)S(1)}, bf16[2,512,2,512]{3,2,1,0:T(2,128)(2,1)}, u32[]{:S(2)}) copy-start(bf16[2,512,2,512]{3,2,1,0:T(2,128)(2,1)} %param.3) | copy-start | bytes 6291460
  69.7 1.9 %copy-start.2 = (bf16[2,2,512,512]{3,2,0,1:T(8,128)(2,1)S(1)}, bf16[2,2,512,512]{3,2,0,1:T(8,128)(2,1)}, u32[]{:S(2)}) copy-start(bf16[2,2,512,512]{3,2,0,1:T(8,128)(2,1)} %all-gather.3.cloned.1.call-done) | copy-start | bytes 6291460
  71.6 1.6 copy-start.3
  71.6 1.9 %copy-start.4 = (bf16[2,512,1,512]{1,3,0,2:T(8,128)(2,1)S(1)}, bf16[2,512,1,512]{1,3,0,2:T(8,128)(2,1)}, u32[]{:S(2)}) copy-start(bf16[2,512,1,512]{1,3,0,2:T(8,128)(2,1)} %copy.14) | copy-start | bytes 3145732
  127.7 2.2 %copy-start.1 = (bf16[2,2,512,512]{3,2,0,1:T(8,128)(2,1)S(1)}, bf16[2,2,512,512]{3,2,0,1:T(8,128)(2,1)}, u32[]{:S(2)}) copy-start(bf16[2,2,512,512]{3,2,0,1:T(8,128)(2,1)} %all-gather.5.cloned.1.call-done) | copy-start | bytes 6291460
  129.9 1.2 copy-start.5
Sparse Core Ops, SparseCore 0:
  10.9 58.8 all-gather.2
  72.6 55.0 all-gather.4
where the time goes:
time: 181 us; the launch traced here: 180 us
  blocking collectives  78 us (43%)
  waiting for transfers between devices  49.1 us (27%)
  local copies, waits for them, and re-layouts  28.4 us (16%)
  between operations  14.1 us (8%)
  other arithmetic  5.51 us (3%)
  matrix products  5.19 us (3%)
    pmax x2, blocking collectives, body(): lax.pmax((jnp.max(single_b, axis=1), jnp.max(single_m, axis=1)), 'grid')  78 us
    all_gather x1, waiting for transfers between devices, body(): power = add_form(lax.all_gather(csm, 'grid', axis=2, tiled=True))  36.6 us
    unnamed x16, local copies, waits for them, and re-layouts  17 us
    all_gather x1, waiting for transfers between devices, body(): quad = add_form(lax.all_gather(inverse, 'grid', axis=2, tiled=True))  12.4 us
    dot_general x2, matrix products, add_form(): jnp.einsum('fgn,fkn->fgk', wide_bf, block, preferred_element_type=jnp.flo...  5.19 us
    reshape x1, local copies, waits for them, and re-layouts, body(): wide_bf = replicas.reshape(bins, points, 2 * width)  4.59 us
    slice x1, local copies, waits for them, and re-layouts, body(): real_vec = replicas[:, :, 0, :]  4.23 us
  transfers between devices with their start and end apart: 2, of which 2 were waited for; matrix products, arithmetic and copies ran while one was open for 16% of the time, Pallas kernels for 0%

commit v1 on v0

v1 whole, which is shorter than its diff:
```python
import functools

import jax
import jax.numpy as jnp
from jax import lax
from jax.experimental import pallas as pl
from jax.experimental.pallas import tpu as pltpu
from jax.sharding import PartitionSpec as P

GROUP = 8


def kernel(
    n, total_bins, rep_hbm, csm_ref, inv_ref, bart_ref, mvdr_ref,
    held, vecs, even, odd, mine, peaks, rep_sem, send_sem, recv_sem, out_sem, in_sem,
):
    bins, points, _, width = rep_hbm.shape
    rows = csm_ref.shape[2]
    half = width // 2
    far = n // GROUP
    me = lax.axis_index("grid")
    core = lax.rem(me, 2)
    low = lax.rem(me, GROUP)
    level = me // GROUP

    def flipped(index, bit):
        return index + bit * (1 - 2 * lax.rem(index // bit, 2))

    first = 2 + 2 * core
    second = 6 - first
    other = me + 1 - 2 * core
    across_a = flipped(me, first)
    across_b = flipped(me, second)
    stacked = [lax.rem(level + step, far) * GROUP + low for step in range(1, far)]

    barrier = pltpu.get_barrier_semaphore()
    for peer in [other, across_a, across_b] + stacked:
        pl.semaphore_signal(barrier, inc=1, device_id={"grid": peer})

    loads = []
    for f in range(bins):
        load = pltpu.make_async_copy(rep_hbm.at[f], vecs.at[f], rep_sem.at[f])
        load.start()
        loads.append(load)

    row_at = lax.broadcasted_iota(jnp.int32, (rows, width), 0) + me * rows
    col_at = lax.broadcasted_iota(jnp.int32, (rows, width), 1)
    upper = jnp.where(col_at > row_at, 1.0, jnp.where(col_at == row_at, 0.5, 0.0))
    lower = jnp.where(col_at < row_at, 1.0, 0.0)
    for m, ref in enumerate((csm_ref, inv_ref)):
        for f in range(bins):
            real = ref[f, 0].astype(jnp.float32)
            imag = ref[f, 1].astype(jnp.float32)
            held[m, me, f] = (real * upper + imag * lower).astype(jnp.bfloat16)

    pl.semaphore_wait(barrier, 2 + far)

    sends = []

    def send(m, owner, peer):
        k = len(sends)
        copy = pltpu.make_async_remote_copy(
            src_ref=held.at[m, owner],
            dst_ref=held.at[m, owner],
            send_sem=send_sem.at[k],
            recv_sem=recv_sem.at[m, owner],
            device_id={"grid": peer},
        )
        copy.start()
        sends.append(copy)

    def arrive(m, owner):
        pltpu.make_async_copy(held.at[m, owner], held.at[m, owner], recv_sem.at[m, owner]).wait()

    def split(f):
        loads[f].wait()
        block = min(points, 128)
        at = lax.broadcasted_iota(jnp.int32, (2 * block, 2 * block), 0)
        source = lax.broadcasted_iota(jnp.int32, (2 * block, 2 * block), 1)
        wanted = jnp.where(at < block, 2 * at, 2 * (at - block) + 1)
        pick = jnp.where(source == wanted, 1.0, 0.0).astype(jnp.bfloat16)

        def step(b, carry):
            where = pl.ds(pl.multiple_of(b * block, block), block)
            mixed = vecs[f, where].reshape(2 * block, width)
            apart = jnp.dot(pick, mixed, preferred_element_type=jnp.float32)
            re = apart[:block].astype(jnp.bfloat16)
            im = apart[block:].astype(jnp.bfloat16)
            for h in range(2):
                cols = slice(h * half, (h + 1) * half)
                even[f, where, 2 * h * half:(2 * h + 1) * half] = im[:, cols]
                even[f, where, (2 * h + 1) * half:(2 * h + 2) * half] = re[:, cols]
                odd[f, where, 2 * h * half:(2 * h + 1) * half] = -re[:, cols]
                odd[f, where, (2 * h + 1) * half:(2 * h + 2) * half] = im[:, cols]
            return carry

        lax.fori_loop(0, points // block, step, 0)

    lanes = 128
    ones = jnp.ones((8, lanes), jnp.float32)

    def fold(value):
        total = value[:, :lanes]
        for k in range(1, value.shape[1] // lanes):
            total = total + value[:, k * lanes:(k + 1) * lanes]
        return total

    def to_lanes(part):
        return lax.dot_general(
            ones, part, (((1,), (1,)), ((), ())),
            precision=lax.Precision.HIGHEST, preferred_element_type=jnp.float32,
        )[0:1]

    def energy_of(f):
        wide = even[f].astype(jnp.float32)
        return to_lanes(fold(wide * wide)) + 1e-06

    tri_row = lax.broadcasted_iota(jnp.int32, (half, half), 0)
    tri_col = lax.broadcasted_iota(jnp.int32, (half, half), 1)
    keep_up = jnp.where(tri_col >= tri_row, 1.0, 0.0).astype(jnp.bfloat16)
    keep_low = jnp.where(tri_col < tri_row, 1.0, 0.0).astype(jnp.bfloat16)

    def form(m, f):
        whole = held[m, :, f].reshape(width, width)
        p00, p01 = whole[:half, :half], whole[:half, half:]
        p10, p11 = whole[half:, :half], whole[half:, half:]
        left = jnp.concatenate([p00 * keep_low, p00 * keep_up, p10], axis=0)
        right = jnp.concatenate([p01, p11 * keep_low, p11 * keep_up], axis=0)
        outs = []
        step = min(points, 256)
        for b in range(points // step):
            where = slice(b * step, (b + 1) * step)
            total = None
            for ref, weigh in ((even, 1), (odd, 1)):
                for h, mat in enumerate((left, right)):
                    image = jnp.dot(
                        ref[f, where, h * half:h * half + 3 * half], mat,
                        preferred_element_type=jnp.float32,
                    )
                    match = ref[f, where, (2 * h + 1) * half:(2 * h + 2) * half]
                    term = fold(image * match.astype(jnp.float32))
                    total = term if total is None else total + term
            outs.append(to_lanes(total))
        return 2.0 * jnp.concatenate(outs, axis=1)

    owners_z = [lax.rem(level + far - step, far) * GROUP + low for step in range(1, far)]
    column = [me] + owners_z
    column_a = [flipped(o, first) for o in column]
    column_b = [flipped(o, second) for o in column]
    column_ab = [flipped(o, second) for o in column_a]

    for m in range(2):
        for peer in [across_a, across_b] + stacked + [other]:
            send(m, me, peer)

    split(0)
    for m in range(2):
        for owner in owners_z:
            arrive(m, owner)
            for peer in (across_a, across_b, other):
                send(m, owner, peer)
    for f in range(1, bins):
        split(f)
    energies = [energy_of(f) for f in range(bins)]
    for m in range(2):
        for owner in column_a:
            arrive(m, owner)
            send(m, owner, across_b)
            send(m, owner, other)

    def finish(m):
        for owner in column_b + column_ab:
            arrive(m, owner)
            send(m, owner, other)

    def partner(m):
        for owner in column + column_a + column_b + column_ab:
            arrive(m, owner + 1 - 2 * core)

    finish(0)
    partner(0)
    single = [form(0, f) / energies[f] for f in range(bins)]
    finish(1)
    partner(1)
    single += [energies[f] / form(1, f) for f in range(bins)]

    for k, value in enumerate(single):
        mine[k:k + 1] = jnp.broadcast_to(jnp.max(value, axis=1, keepdims=True), (1, lanes))

    shouts = []
    for step in range(1, n):
        copy = pltpu.make_async_remote_copy(
            src_ref=mine,
            dst_ref=peaks.at[step - 1],
            send_sem=out_sem.at[step - 1],
            recv_sem=in_sem.at[step - 1],
            device_id={"grid": lax.rem(me + step, n)},
        )
        copy.start()
        shouts.append(copy)
    for copy in sends:
        copy.wait_send()
    for copy in shouts:
        copy.wait_recv()
    top = jnp.maximum(jnp.max(peaks[...], axis=0), mine[...])
    for ref, at in ((bart_ref, 0), (mvdr_ref, bins)):
        total = None
        for f in range(bins):
            term = single[at + f] / top[at + f:at + f + 1, 0:1]
            total = term if total is None else total + term
        ref[...] = total / total_bins
    for copy in shouts:
        copy.wait_send()


def body(n, replicas, csm, inverse):
    bins, points, _, width = replicas.shape
    rows = csm.shape[2]
    over = lax.axis_size("freq")
    far = n // GROUP
    copies = 2 * (n - 1)
    vmem = pl.BlockSpec(memory_space=pltpu.VMEM)
    bart, mvdr = pl.pallas_call(
        functools.partial(kernel, n, bins * over),
        out_shape=[jax.ShapeDtypeStruct((1, points), jnp.float32)] * 2,
        in_specs=[pl.BlockSpec(memory_space=pl.ANY), vmem, vmem],
        out_specs=[vmem, vmem],
        scratch_shapes=[
            pltpu.VMEM((2, n, bins, rows, width), jnp.bfloat16),
            pltpu.VMEM((bins, points, 2, width), jnp.bfloat16),
            pltpu.VMEM((bins, points, 2 * width), jnp.bfloat16),
            pltpu.VMEM((bins, points, 2 * width), jnp.bfloat16),
            pltpu.VMEM((2 * bins, 128), jnp.float32),
            pltpu.VMEM((n - 1, 2 * bins, 128), jnp.float32),
            pltpu.SemaphoreType.DMA((bins,)),
            pltpu.SemaphoreType.DMA((copies,)),
            pltpu.SemaphoreType.DMA((2, n)),
            pltpu.SemaphoreType.DMA((n - 1,)),
            pltpu.SemaphoreType.DMA((n - 1,)),
        ],
        compiler_params=pltpu.CompilerParams(
            collective_id=0, has_side_effects=True, vmem_limit_bytes=48 * 1024 * 1024
        ),
    )(replicas, csm, inverse)
    if over == 1:
        return bart.reshape(points), mvdr.reshape(points)
    whole = lax.psum(jnp.concatenate([bart, mvdr], axis=0), "freq")
    share = points // over
    summed = lax.dynamic_slice_in_dim(whole, lax.axis_index("freq") * share, share, 1)
    return summed[0], summed[1]


def solution(mesh):
    in_specs = (
        P("freq", "grid", None, None),
        P("freq", None, "grid", None),
        P("freq", None, "grid", None),
    )
    out_specs = (P(("grid", "freq")), P(("grid", "freq")))
    return jax.shard_map(
        functools.partial(body, mesh.shape["grid"]),
        mesh=mesh, in_specs=in_specs, out_specs=out_specs, check_vma=False,
    )
```

time: 181 us -> 38.5 us (0.21)
  blocking collectives: 78 us -> 0 us
  waiting for transfers between devices: 49.1 us -> 0 us
  Pallas kernels: 0 us -> 33.2 us
  local copies, waits for them, and re-layouts: 28.4 us -> 4.42 us
  between operations: 14.1 us -> 0.65 us
  other arithmetic: 5.51 us -> 0 us
  matrix products: 5.19 us -> 0 us
    pmax x2 -> x0, blocking collectives: 78 us -> none  [body(): lax.pmax((jnp.max(single_b, axis=1), jnp.max(single_m, axis=1)), 'grid')]
    all_gather x2 -> x0, waiting for transfers between devices: 49 us -> none  [the longest x1 36.6 us: body(): power = add_form(lax.all_gather(csm, 'grid', axis=2, tiled=True))]
    pallas_call x0 -> x1, Pallas kernels: none -> 33.2 us  [body(): pl.pallas_call(functools.partial(kernel, n, bins * over), out_shape=[jax....]
    unnamed x16 -> x8, local copies, waits for them, and re-layouts: 17 us -> 4.42 us
    dot_general x2 -> x0, matrix products: 5.19 us -> none  [add_form(): jnp.einsum('fgn,fkn->fgk', wide_bf, block, preferred_element_type=jnp.flo...]
    slice x2 -> x0, local copies, waits for them, and re-layouts: 4.82 us -> none  [the longest x1 4.23 us: body(): real_vec = replicas[:, :, 0, :]]
    reshape x1 -> x0, local copies, waits for them, and re-layouts: 4.59 us -> none  [body(): wide_bf = replicas.reshape(bins, points, 2 * width)]
    reduce_sum x3 -> x0, other arithmetic: 3.86 us -> none  [the longest x1 3.62 us: body(): energy = jnp.sum(wide * wide, axis=2) + 1e-06]
  transfers between devices with their start and end apart: 2 -> 0, of which waited for: 2 -> 0; matrix products, arithmetic and copies ran while one was open for 16% -> 0% of each run, Pallas kernels for 0% -> 0%
where the time goes in v1:
time: 38.5 us; the launch traced here: 38.3 us
  Pallas kernels  33.2 us (86%)
  local copies, waits for them, and re-layouts  4.42 us (11%)
  between operations  0.65 us (2%)
    pallas_call x1, Pallas kernels, body(): pl.pallas_call(functools.partial(kernel, n, bins * over), out_shape=[jax....  33.2 us
    unnamed x8, local copies, waits for them, and re-layouts  4.42 us

profile of v1, /device:TPU:0, one launch (start us, length us, event | category | flops | bytes accessed | tf_op | source)
XLA Modules:
  0.0 38.3 jit_solution(15397502765725980353)
XLA Ops:
  0.6 0.0 copy-start
  0.6 1.6 %copy-done = bf16[2,512,2,512]{3,2,1,0:T(2,128)(2,1)S(1)} copy-done((bf16[2,512,2,512]{3,2,1,0:T(2,128)(2,1)S(1)}, bf16[2,512,2,512]{3,2,1,0:T(2,128)(2,1)}, u32[]{:S(2)}) %copy-start) | copy-done | bytes 2097176
  2.2 0.0 copy-start.1
  2.2 0.8 %copy-done.1 = bf16[2,2,16,512]{3,2,1,0:T(8,128)(2,1)S(1)} copy-done((bf16[2,2,16,512]{3,2,1,0:T(8,128)(2,1)S(1)}, bf16[2,2,16,512]{3,2,1,0:T(8,128)(2,1)}, u32[]{:S(2)}) %copy-start.1) | copy-done | bytes 65560
  3.1 0.0 copy-start.2
  3.1 0.8 %copy-done.2 = bf16[2,2,16,512]{3,2,1,0:T(8,128)(2,1)S(1)} copy-done((bf16[2,2,16,512]{3,2,1,0:T(8,128)(2,1)S(1)}, bf16[2,2,16,512]{3,2,1,0:T(8,128)(2,1)}, u32[]{:S(2)}) %copy-start.2) | copy-done | bytes 65560
  3.9 33.2 %shard_map.50 = (f32[1,512]{1,0:T(1,128)S(1)}, f32[1,512]{1,0:T(1,128)S(1)}) custom-call(bf16[2,512,2,512]{3,2,1,0:T(2,128)(2,1)S(1)} %copy-done, bf16[2,2,16,512]{3,2,1,0:T(8,128)(2,1)S(1)} %copy-done.1, bf16[2,2,16,512]{3,2,1,0:T(8,128)(2,1)S(1)} %copy-done.2), custom_call_target="tpu_custom_call" | custom-call | tf_op jit(solution)/shard_map/pallas_call | solution.py:223
  37.1 0.6 %copy.7 = f32[512]{0:T(512)} copy(f32[512]{0:T(512)S(1)} %bitcast.3) | data formatting | bytes 4096
  37.7 0.6 %copy.8 = f32[512]{0:T(512)} copy(f32[512]{0:T(512)S(1)} %bitcast.2) | data formatting | bytes 4096
Async XLA Ops:
  0.6 1.6 %copy-start = (bf16[2,512,2,512]{3,2,1,0:T(2,128)(2,1)S(1)}, bf16[2,512,2,512]{3,2,1,0:T(2,128)(2,1)}, u32[]{:S(2)}) copy-start(bf16[2,512,2,512]{3,2,1,0:T(2,128)(2,1)} %rep_hbm.1) | copy-start | bytes 6291460
  2.2 0.8 %copy-start.1 = (bf16[2,2,16,512]{3,2,1,0:T(8,128)(2,1)S(1)}, bf16[2,2,16,512]{3,2,1,0:T(8,128)(2,1)}, u32[]{:S(2)}) copy-start(bf16[2,2,16,512]{3,2,1,0:T(8,128)(2,1)} %csm_ref.1) | copy-start | bytes 196612
  3.1 0.8 %copy-start.2 = (bf16[2,2,16,512]{3,2,1,0:T(8,128)(2,1)S(1)}, bf16[2,2,16,512]{3,2,1,0:T(8,128)(2,1)}, u32[]{:S(2)}) copy-start(bf16[2,2,16,512]{3,2,1,0:T(8,128)(2,1)} %inv_ref.1) | copy-start | bytes 196612

commit v2 on v1

--- a/solution.py
+++ b/solution.py
@@ -11,11 +11,11 @@
 
 
 def kernel(
-    n, total_bins, rep_hbm, csm_ref, inv_ref, bart_ref, mvdr_ref,
-    held, vecs, even, odd, mine, peaks, rep_sem, send_sem, recv_sem, out_sem, in_sem,
+    n, total_bins, rep_hbm, csm_hbm, inv_hbm, out_ref,
+    held, vecs, slabs, even, odd, mine, peaks, rep_sem, slab_sem, send_sem, recv_sem, out_sem, in_sem,
 ):
     bins, points, _, width = rep_hbm.shape
-    rows = csm_ref.shape[2]
+    rows = csm_hbm.shape[2]
     half = width // 2
     far = n // GROUP
     me = lax.axis_index("grid")
@@ -33,6 +33,12 @@
     across_b = flipped(me, second)
     stacked = [lax.rem(level + step, far) * GROUP + low for step in range(1, far)]
 
+    pieces = []
+    for m, ref in enumerate((csm_hbm, inv_hbm)):
+        piece = pltpu.make_async_copy(ref, slabs.at[m], slab_sem.at[m])
+        piece.start()
+        pieces.append(piece)
+
     barrier = pltpu.get_barrier_semaphore()
     for peer in [other, across_a, across_b] + stacked:
         pl.semaphore_signal(barrier, inc=1, device_id={"grid": peer})
@@ -47,10 +53,11 @@
     col_at = lax.broadcasted_iota(jnp.int32, (rows, width), 1)
     upper = jnp.where(col_at > row_at, 1.0, jnp.where(col_at == row_at, 0.5, 0.0))
     lower = jnp.where(col_at < row_at, 1.0, 0.0)
-    for m, ref in enumerate((csm_ref, inv_ref)):
+    for m in range(2):
+        pieces[m].wait()
         for f in range(bins):
-            real = ref[f, 0].astype(jnp.float32)
-            imag = ref[f, 1].astype(jnp.float32)
+            real = slabs[m, f, 0].astype(jnp.float32)
+            imag = slabs[m, f, 1].astype(jnp.float32)
             held[m, me, f] = (real * upper + imag * lower).astype(jnp.bfloat16)
 
     pl.semaphore_wait(barrier, 2 + far)
@@ -127,7 +134,7 @@
         left = jnp.concatenate([p00 * keep_low, p00 * keep_up, p10], axis=0)
         right = jnp.concatenate([p01, p11 * keep_low, p11 * keep_up], axis=0)
         outs = []
-        step = min(points, 256)
+        step = min(points, 512)
         for b in range(points // step):
             where = slice(b * step, (b + 1) * step)
             total = None
@@ -153,23 +160,20 @@
         for peer in [across_a, across_b] + stacked + [other]:
             send(m, me, peer)
 
-    split(0)
-    for m in range(2):
+    def pass_z(m):
         for owner in owners_z:
             arrive(m, owner)
-            for peer in (across_a, across_b, other):
+            for peer in (across_b, across_a, other):
                 send(m, owner, peer)
-    for f in range(1, bins):
-        split(f)
-    energies = [energy_of(f) for f in range(bins)]
-    for m in range(2):
+
+    def pass_a(m):
         for owner in column_a:
             arrive(m, owner)
             send(m, owner, across_b)
             send(m, owner, other)
 
-    def finish(m):
-        for owner in column_b + column_ab:
+    def pass_b(m, owners):
+        for owner in owners:
             arrive(m, owner)
             send(m, owner, other)
 
@@ -177,10 +181,20 @@
         for owner in column + column_a + column_b + column_ab:
             arrive(m, owner + 1 - 2 * core)
 
-    finish(0)
+    split(0)
+    pass_z(0)
+    for f in range(1, bins):
+        split(f)
+    energies = [energy_of(f) for f in range(bins)]
+    pass_a(0)
+    pass_z(1)
+    pass_b(0, column_b + column_ab)
+    pass_a(1)
     partner(0)
-    single = [form(0, f) / energies[f] for f in range(bins)]
-    finish(1)
+    single = [form(0, 0) / energies[0]]
+    pass_b(1, column_b)
+    single += [form(0, f) / energies[f] for f in range(1, bins)]
+    pass_b(1, column_ab)
     partner(1)
     single += [energies[f] / form(1, f) for f in range(bins)]
 
@@ -203,12 +217,13 @@
     for copy in shouts:
         copy.wait_recv()
     top = jnp.maximum(jnp.max(peaks[...], axis=0), mine[...])
-    for ref, at in ((bart_ref, 0), (mvdr_ref, bins)):
+    for row in range(2):
+        at = row * bins
         total = None
         for f in range(bins):
             term = single[at + f] / top[at + f:at + f + 1, 0:1]
             total = term if total is None else total + term
-        ref[...] = total / total_bins
+        out_ref[row:row + 1] = total / total_bins
     for copy in shouts:
         copy.wait_send()
 
@@ -219,32 +234,33 @@
     over = lax.axis_size("freq")
     far = n // GROUP
     copies = 2 * (n - 1)
-    vmem = pl.BlockSpec(memory_space=pltpu.VMEM)
-    bart, mvdr = pl.pallas_call(
+    whole = pl.pallas_call(
         functools.partial(kernel, n, bins * over),
-        out_shape=[jax.ShapeDtypeStruct((1, points), jnp.float32)] * 2,
-        in_specs=[pl.BlockSpec(memory_space=pl.ANY), vmem, vmem],
-        out_specs=[vmem, vmem],
+        out_shape=jax.ShapeDtypeStruct((2, points), jnp.float32),
+        in_specs=[pl.BlockSpec(memory_space=pltpu.HBM)] * 3,
+        out_specs=pl.BlockSpec(memory_space=pltpu.VMEM),
         scratch_shapes=[
             pltpu.VMEM((2, n, bins, rows, width), jnp.bfloat16),
             pltpu.VMEM((bins, points, 2, width), jnp.bfloat16),
+            pltpu.VMEM((2, bins, 2, rows, width), jnp.bfloat16),
             pltpu.VMEM((bins, points, 2 * width), jnp.bfloat16),
             pltpu.VMEM((bins, points, 2 * width), jnp.bfloat16),
             pltpu.VMEM((2 * bins, 128), jnp.float32),
             pltpu.VMEM((n - 1, 2 * bins, 128), jnp.float32),
             pltpu.SemaphoreType.DMA((bins,)),
+            pltpu.SemaphoreType.DMA((2,)),
             pltpu.SemaphoreType.DMA((copies,)),
             pltpu.SemaphoreType.DMA((2, n)),
             pltpu.SemaphoreType.DMA((n - 1,)),
             pltpu.SemaphoreType.DMA((n - 1,)),
         ],
         compiler_params=pltpu.CompilerParams(
-            collective_id=0, has_side_effects=True, vmem_limit_bytes=48 * 1024 * 1024
+            collective_id=0, has_side_effects=True, vmem_limit_bytes=67043328
         ),
     )(replicas, csm, inverse)
     if over == 1:
-        return bart.reshape(points), mvdr.reshape(points)
-    whole = lax.psum(jnp.concatenate([bart, mvdr], axis=0), "freq")
+        return whole[0], whole[1]
+    whole = lax.psum(whole, "freq")
     share = points // over
     summed = lax.dynamic_slice_in_dim(whole, lax.axis_index("freq") * share, share, 1)
     return summed[0], summed[1]

time: 38.5 us -> 34.3 us (0.89)
  local copies, waits for them, and re-layouts: 4.42 us -> 1.33 us
  Pallas kernels: 33.2 us -> 32.1 us
    unnamed x8 -> x0, local copies, waits for them, and re-layouts: 4.42 us -> none
    slice x0 -> x1, local copies, waits for them, and re-layouts: none -> 1.33 us  [body(): return (whole[0], whole[1])]
    pallas_call x1, Pallas kernels: 33.2 us -> 32.1 us  [body(): pl.pallas_call(functools.partial(kernel, n, bins * over), out_shape=jax.S...]
where the time goes in v2:
time: 34.3 us; the launch traced here: 34.1 us
  Pallas kernels  32.1 us (94%)
  local copies, waits for them, and re-layouts  1.33 us (4%)
  between operations  0.64 us (2%)
    pallas_call x1, Pallas kernels, body(): pl.pallas_call(functools.partial(kernel, n, bins * over), out_shape=jax.S...  32.1 us
    slice x1, local copies, waits for them, and re-layouts, body(): return (whole[0], whole[1])  1.33 us

profile of v2, /device:TPU:0, one launch (start us, length us, event | category | flops | bytes accessed | tf_op | source)
XLA Modules:
  0.0 34.1 jit_solution(6429126979235879768)
XLA Ops:
  0.6 32.1 %shard_map.50 = f32[2,512]{1,0:T(2,128)} custom-call(bf16[2,512,2,512]{3,2,1,0:T(2,128)(2,1)} %rep_hbm.1, bf16[2,2,16,512]{3,2,1,0:T(8,128)(2,1)} %csm_hbm.1, bf16[2,2,16,512]{3,2,1,0:T(8,128)(2,1)} %inv_hbm.1), custom_call_target="tpu_custom_call" | custom-call | tf_op jit(solution)/shard_map/pallas_call | solution.py:237
  32.7 1.3 %fusion = (f32[1,512]{1,0:T(1,128)}, f32[1,512]{1,0:T(1,128)}) fusion(f32[2,512]{1,0:T(2,128)} %shard_map.50), kind=kLoop, calls=%fused_computation | loop fusion | bytes 8192 | tf_op jit(solution)/shard_map/slice | solution.py:262

commit v3 on v2

--- a/solution.py
+++ b/solution.py
@@ -12,11 +12,11 @@
 
 def kernel(
     n, total_bins, rep_hbm, csm_hbm, inv_hbm, out_ref,
-    held, vecs, slabs, even, odd, mine, peaks, rep_sem, slab_sem, send_sem, recv_sem, out_sem, in_sem,
+    held, vecs, slabs, natural, even, odd, ups, lows, parts, mine, peaks, rep_sem, slab_sem, send_sem, recv_sem, out_sem, in_sem,
 ):
     bins, points, _, width = rep_hbm.shape
     rows = csm_hbm.shape[2]
-    half = width // 2
+    wide = width // 4
     far = n // GROUP
     me = lax.axis_index("grid")
     core = lax.rem(me, 2)
@@ -58,7 +58,7 @@
         for f in range(bins):
             real = slabs[m, f, 0].astype(jnp.float32)
             imag = slabs[m, f, 1].astype(jnp.float32)
-            held[m, me, f] = (real * upper + imag * lower).astype(jnp.bfloat16)
+            held[m * bins + f, me] = (real * upper + imag * lower).astype(jnp.bfloat16)
 
     pl.semaphore_wait(barrier, 2 + far)
 
@@ -79,6 +79,25 @@
     def arrive(m, owner):
         pltpu.make_async_copy(held.at[m, owner], held.at[m, owner], recv_sem.at[m, owner]).wait()
 
+    owners_z = [lax.rem(level + far - step, far) * GROUP + low for step in range(1, far)]
+    column = [me] + owners_z
+    column_a = [flipped(o, first) for o in column]
+    column_b = [flipped(o, second) for o in column]
+    column_ab = [flipped(o, second) for o in column_a]
+    across = [[o + 1 - 2 * core for o in part] for part in (column, column_b, column_a, column_ab)]
+    groups = [
+        column + across[0], column_a + across[1], column_b + across[2], column_ab + across[3]
+    ]
+    order = [owner for group in groups for owner in group]
+
+    def element(shape, axis):
+        at = lax.broadcasted_iota(jnp.int32, shape, axis)
+        inside = lax.rem(at, rows)
+        found = inside
+        for k, owner in enumerate(order):
+            found = jnp.where((at >= k * rows) & (at < (k + 1) * rows), owner * rows + inside, found)
+        return found
+
     def split(f):
         loads[f].wait()
         block = min(points, 128)
@@ -93,12 +112,16 @@
             apart = jnp.dot(pick, mixed, preferred_element_type=jnp.float32)
             re = apart[:block].astype(jnp.bfloat16)
             im = apart[block:].astype(jnp.bfloat16)
-            for h in range(2):
-                cols = slice(h * half, (h + 1) * half)
-                even[f, where, 2 * h * half:(2 * h + 1) * half] = im[:, cols]
-                even[f, where, (2 * h + 1) * half:(2 * h + 2) * half] = re[:, cols]
-                odd[f, where, 2 * h * half:(2 * h + 1) * half] = -re[:, cols]
-                odd[f, where, (2 * h + 1) * half:(2 * h + 2) * half] = im[:, cols]
+            natural[f, 0, where] = re
+            natural[f, 1, where] = im
+            re = jnp.dot(re, moved, preferred_element_type=jnp.float32).astype(jnp.bfloat16)
+            im = jnp.dot(im, moved, preferred_element_type=jnp.float32).astype(jnp.bfloat16)
+            for g in range(4):
+                cols = slice(g * wide, (g + 1) * wide)
+                even[f, where, 2 * g * wide:(2 * g + 1) * wide] = re[:, cols]
+                even[f, where, (2 * g + 1) * wide:(2 * g + 2) * wide] = im[:, cols]
+                odd[f, where, 2 * g * wide:(2 * g + 1) * wide] = im[:, cols]
+                odd[f, where, (2 * g + 1) * wide:(2 * g + 2) * wide] = -re[:, cols]
             return carry
 
         lax.fori_loop(0, points // block, step, 0)
@@ -119,45 +142,27 @@
         )[0:1]
 
     def energy_of(f):
-        wide = even[f].astype(jnp.float32)
-        return to_lanes(fold(wide * wide)) + 1e-06
-
-    tri_row = lax.broadcasted_iota(jnp.int32, (half, half), 0)
-    tri_col = lax.broadcasted_iota(jnp.int32, (half, half), 1)
-    keep_up = jnp.where(tri_col >= tri_row, 1.0, 0.0).astype(jnp.bfloat16)
-    keep_low = jnp.where(tri_col < tri_row, 1.0, 0.0).astype(jnp.bfloat16)
-
-    def form(m, f):
-        whole = held[m, :, f].reshape(width, width)
-        p00, p01 = whole[:half, :half], whole[:half, half:]
-        p10, p11 = whole[half:, :half], whole[half:, half:]
-        left = jnp.concatenate([p00 * keep_low, p00 * keep_up, p10], axis=0)
-        right = jnp.concatenate([p01, p11 * keep_low, p11 * keep_up], axis=0)
-        outs = []
-        step = min(points, 512)
-        for b in range(points // step):
-            where = slice(b * step, (b + 1) * step)
-            total = None
-            for ref, weigh in ((even, 1), (odd, 1)):
-                for h, mat in enumerate((left, right)):
-                    image = jnp.dot(
-                        ref[f, where, h * half:h * half + 3 * half], mat,
-                        preferred_element_type=jnp.float32,
-                    )
-                    match = ref[f, where, (2 * h + 1) * half:(2 * h + 2) * half]
-                    term = fold(image * match.astype(jnp.float32))
-                    total = term if total is None else total + term
-            outs.append(to_lanes(total))
-        return 2.0 * jnp.concatenate(outs, axis=1)
-
-    owners_z = [lax.rem(level + far - step, far) * GROUP + low for step in range(1, far)]
-    column = [me] + owners_z
-    column_a = [flipped(o, first) for o in column]
-    column_b = [flipped(o, second) for o in column]
-    column_ab = [flipped(o, second) for o in column_a]
-
-    for m in range(2):
-        for peer in [across_a, across_b] + stacked + [other]:
+        re = natural[f, 0].astype(jnp.float32)
+        im = natural[f, 1].astype(jnp.float32)
+        return to_lanes(fold(re * re) + fold(im * im)) + 1e-06
+
+    def work(m, g):
+        f = m % bins
+        block = jnp.concatenate([held[m, owner] for owner in groups[g]], axis=0)
+        cols = slice(g * wide, (g + 1) * wide)
+        mat = jnp.concatenate([block * ups[cols], block * lows[cols]], axis=0)
+        total = None
+        for ref, k in ((even, 0), (odd, 1)):
+            image = jnp.dot(
+                ref[f, :, 2 * g * wide:(2 * g + 2) * wide], mat, preferred_element_type=jnp.float32
+            )
+            term = fold(image * natural[f, k].astype(jnp.float32))
+            total = term if total is None else total + term
+        parts[m] = total if g == 0 else parts[m] + total
+
+    phases = range(2 * bins)
+    for m in phases:
+        for peer in [across_b, across_a] + stacked + [other]:
             send(m, me, peer)
 
     def pass_z(m):
@@ -177,26 +182,47 @@
             arrive(m, owner)
             send(m, owner, other)
 
-    def partner(m):
-        for owner in column + column_a + column_b + column_ab:
-            arrive(m, owner + 1 - 2 * core)
-
+    def partner(m, g):
+        for owner in across[g]:
+            arrive(m, owner)
+
+    spot = element((8, width), 1)[0:1]
+    moved = jnp.where(
+        lax.broadcasted_iota(jnp.int32, (width, width), 0) == spot, 1.0, 0.0
+    ).astype(jnp.bfloat16)
     split(0)
-    pass_z(0)
+    for m in phases:
+        pass_z(m)
     for f in range(1, bins):
         split(f)
+    rank = element((width, 128), 0)
+    for k in range(width // 128):
+        cols = slice(k * 128, (k + 1) * 128)
+        lane = lax.broadcasted_iota(jnp.int32, (width, 128), 1) + k * 128
+        ups[:, cols] = jnp.where(lane >= rank, 1.0, 0.0).astype(jnp.bfloat16)
+        lows[:, cols] = jnp.where(lane < rank, 1.0, 0.0).astype(jnp.bfloat16)
+    for m in phases:
+        pass_a(m)
+        pass_b(m, column_b)
     energies = [energy_of(f) for f in range(bins)]
-    pass_a(0)
-    pass_z(1)
-    pass_b(0, column_b + column_ab)
-    pass_a(1)
-    partner(0)
-    single = [form(0, 0) / energies[0]]
-    pass_b(1, column_b)
-    single += [form(0, f) / energies[f] for f in range(1, bins)]
-    pass_b(1, column_ab)
-    partner(1)
-    single += [energies[f] / form(1, f) for f in range(bins)]
+    for m in phases:
+        partner(m, 0)
+        work(m, 0)
+    for m in phases:
+        pass_b(m, column_ab)
+        partner(m, 1)
+        work(m, 1)
+        partner(m, 2)
+        work(m, 2)
+    single = []
+    for m in phases:
+        partner(m, 3)
+        work(m, 3)
+        form = 2.0 * to_lanes(parts[m])
+        if m < bins:
+            single.append(form / energies[m % bins])
+        else:
+            single.append(energies[m % bins] / form)
 
     for k, value in enumerate(single):
         mine[k:k + 1] = jnp.broadcast_to(jnp.max(value, axis=1, keepdims=True), (1, lanes))
@@ -233,24 +259,28 @@
     rows = csm.shape[2]
     over = lax.axis_size("freq")
     far = n // GROUP
-    copies = 2 * (n - 1)
+    copies = 2 * bins * (n - 1)
     whole = pl.pallas_call(
         functools.partial(kernel, n, bins * over),
         out_shape=jax.ShapeDtypeStruct((2, points), jnp.float32),
         in_specs=[pl.BlockSpec(memory_space=pltpu.HBM)] * 3,
         out_specs=pl.BlockSpec(memory_space=pltpu.VMEM),
         scratch_shapes=[
-            pltpu.VMEM((2, n, bins, rows, width), jnp.bfloat16),
+            pltpu.VMEM((2 * bins, n, rows, width), jnp.bfloat16),
             pltpu.VMEM((bins, points, 2, width), jnp.bfloat16),
             pltpu.VMEM((2, bins, 2, rows, width), jnp.bfloat16),
+            pltpu.VMEM((bins, 2, points, width), jnp.bfloat16),
             pltpu.VMEM((bins, points, 2 * width), jnp.bfloat16),
             pltpu.VMEM((bins, points, 2 * width), jnp.bfloat16),
+            pltpu.VMEM((width, width), jnp.bfloat16),
+            pltpu.VMEM((width, width), jnp.bfloat16),
+            pltpu.VMEM((2 * bins, points, 128), jnp.float32),
             pltpu.VMEM((2 * bins, 128), jnp.float32),
             pltpu.VMEM((n - 1, 2 * bins, 128), jnp.float32),
             pltpu.SemaphoreType.DMA((bins,)),
             pltpu.SemaphoreType.DMA((2,)),
             pltpu.SemaphoreType.DMA((copies,)),
-            pltpu.SemaphoreType.DMA((2, n)),
+            pltpu.SemaphoreType.DMA((2 * bins, n)),
             pltpu.SemaphoreType.DMA((n - 1,)),
             pltpu.SemaphoreType.DMA((n - 1,)),
         ],

time: 34.3 us -> 36.1 us (1.052)
  Pallas kernels: 32.1 us -> 33.9 us
    pallas_call x1, Pallas kernels: 32.1 us -> 33.9 us  [body(): pl.pallas_call(functools.partial(kernel, n, bins * over), out_shape=jax.S...]
where the time goes in v3:
time: 36.1 us; the launch traced here: 35.9 us
  Pallas kernels  33.9 us (94%)
  local copies, waits for them, and re-layouts  1.33 us (4%)
  between operations  0.64 us (2%)
    pallas_call x1, Pallas kernels, body(): pl.pallas_call(functools.partial(kernel, n, bins * over), out_shape=jax.S...  33.9 us
    slice x1, local copies, waits for them, and re-layouts, body(): return (whole[0], whole[1])  1.33 us

profile of v3, /device:TPU:0, one launch (start us, length us, event | category | flops | bytes accessed | tf_op | source)
XLA Modules:
  0.0 35.9 jit_solution(7055452370458351888)
XLA Ops:
  0.6 33.9 %shard_map.50 = f32[2,512]{1,0:T(2,128)} custom-call(bf16[2,512,2,512]{3,2,1,0:T(2,128)(2,1)} %rep_hbm.1, bf16[2,2,16,512]{3,2,1,0:T(8,128)(2,1)} %csm_hbm.1, bf16[2,2,16,512]{3,2,1,0:T(8,128)(2,1)} %inv_hbm.1), custom_call_target="tpu_custom_call" | custom-call | tf_op jit(solution)/shard_map/pallas_call | solution.py:263
  34.6 1.3 %fusion = (f32[1,512]{1,0:T(1,128)}, f32[1,512]{1,0:T(1,128)}) fusion(f32[2,512]{1,0:T(2,128)} %shard_map.50), kind=kLoop, calls=%fused_computation | loop fusion | bytes 8192 | tf_op jit(solution)/shard_map/slice | solution.py:292
